TPU v7x, 32 devices: a whole 2x2x4 slice. The times are simulated.
32 devices in a mesh: seq: 8 (over z, x), batch: 4 (over y, core).
Axes of the slice: x: 2, y: 2, z: 4, core: 2. Of those that a mesh axis runs over, the one named last changes fastest.
Arguments:
- tokens: bfloat16 [4, 2048, 2048], P('batch', 'seq'), may hold values from -6 to 6
- lengths: int32 [4, 1], replicated, may hold values from 512 to 2048, as said below
- cotangent: bfloat16 [4, 2048, 2048], P('batch', 'seq'), may hold values from -6 to 6
- ln1_gain: bfloat16 [2048], P(('seq', 'batch')), may hold values from 0.5 to 1.5
- ln1_bias: bfloat16 [2048], P(('seq', 'batch')), may hold values from -1.5 to 1.5
- w_qkv: bfloat16 [2048, 3, 2048], P('seq', None, 'batch'), may hold values from -0.1875 to 0.1875
- qv_bias: bfloat16 [2, 2048], P(None, 'batch'), may hold values from -1.5 to 1.5
- w_out: bfloat16 [2048, 2048], P('batch', 'seq'), may hold values from -0.375 to 0.375
- out_bias: bfloat16 [2048], P(('seq', 'batch')), may hold values from -1.5 to 1.5
- ln2_gain: bfloat16 [2048], P(('seq', 'batch')), may hold values from 0.5 to 1.5
- ln2_bias: bfloat16 [2048], P(('seq', 'batch')), may hold values from -1.5 to 1.5
- w_fc: bfloat16 [2048, 8192], P('seq', 'batch'), may hold values from -0.125 to 0.125
- fc_bias: bfloat16 [8192], P('batch'), may hold values from -1.5 to 1.5
- w_proj: bfloat16 [8192, 2048], P('batch', 'seq'), may hold values from -0.0625 to 0.0625
- proj_bias: bfloat16 [2048], P(('seq', 'batch')), may hold values from -1.5 to 1.5
Outputs:
- block_out: bfloat16 [4, 2048, 2048], P('batch', 'seq')
- grad_tokens: bfloat16 [4, 2048, 2048], P('batch', 'seq')
- grad_ln1_gain: float32 [2048], P(('seq', 'batch'))
- grad_ln1_bias: float32 [2048], P(('seq', 'batch'))
- grad_w_qkv: float32 [2048, 3, 2048], P('seq', None, 'batch')
- grad_qv_bias: float32 [2, 2048], P(None, 'batch')
- grad_w_out: float32 [2048, 2048], P('batch', 'seq')
- grad_out_bias: float32 [2048], P(('seq', 'batch'))
- grad_ln2_gain: float32 [2048], P(('seq', 'batch'))
- grad_ln2_bias: float32 [2048], P(('seq', 'batch'))
- grad_w_fc: float32 [2048, 8192], P('seq', 'batch')
- grad_fc_bias: float32 [8192], P('batch')
- grad_w_proj: float32 [8192, 2048], P('batch', 'seq')
- grad_proj_bias: float32 [2048], P(('seq', 'batch'))
Inputs may be any that keep to these rules, and one draw needn't show every extreme that they name: `lengths`: some sequence has all 2048 slots true and some other has exactly 512.
All inputs are finite; a program needn't handle non-finite values.
Results may differ from a plain program's by a relative error of at most 0.018.
Values may be sent and summed in bfloat16 or wider, within the bound.
No kernel may reach another device: no remote copies, remote signals or barrier semaphores. Data moves between devices by JAX's collectives and lax.ppermute only.
A program may use at most 448 MiB of HBM per device.

v0:
```python
import jax
import jax.numpy as jnp
from jax import lax
from jax.sharding import PartitionSpec as P

HEAD_DIM = 128
WINDOW = 256


def shifted(value, axis, steps):
    count = lax.axis_size(axis)
    initial, last = (max(0, -steps), min(count, count - steps))
    return lax.ppermute(value, axis, [(source, source + steps) for source in range(initial, last)])


def layer_norm(values, gain, shift):
    mean = jnp.mean(values, axis=-1, keepdims=True)
    centered = values - mean
    factor = lax.rsqrt(jnp.mean(centered * centered, axis=-1, keepdims=True) + 1e-05)
    return centered * factor * gain + shift


def gelu_tanh(values):
    return jax.nn.gelu(values, approximate=True)


def allowed_keys(query_pos, key_pos, limit, seq_length):
    later = query_pos[:, None]
    earlier = key_pos[None, :]
    gap = later - earlier
    same = later // seq_length == earlier // seq_length
    live = (earlier % seq_length < limit[:, None]) | (gap == 0)
    return (earlier >= 0) & (gap >= 0) & (gap < WINDOW) & same & live


def limits_of(chain_lengths, chain_pos, seq_length):
    owner = chain_pos // seq_length
    slots = jnp.arange(chain_lengths.shape[1], dtype=jnp.int32)
    match = owner[:, None] == slots[None, :]
    return jnp.sum(jnp.where(match[None], chain_lengths[:, None, :], 0), axis=2)


def bias_total(values):
    return lax.psum(values.astype(jnp.bfloat16), "seq").astype(jnp.float32)


def rows_total(pair):
    return (
        lax.psum_scatter(
            pair[0].astype(jnp.bfloat16), "seq", scatter_dimension=0, tiled=True
        ).astype(jnp.float32),
        lax.psum_scatter(
            pair[1].astype(jnp.bfloat16), "seq", scatter_dimension=1, tiled=True
        ).astype(jnp.float32),
    )


def shards(
    tokens,
    lengths,
    cotangent,
    ln1_gain,
    ln1_bias,
    w_qkv,
    qv_bias,
    w_out,
    out_bias,
    ln2_gain,
    ln2_bias,
    w_fc,
    fc_bias,
    w_proj,
    proj_bias,
):
    floaty = jnp.float32
    brain = jnp.bfloat16
    rows = tokens.shape[1]
    width = tokens.shape[2]
    head_dim = HEAD_DIM
    scale = head_dim ** (-0.5)
    seq_length = rows * lax.axis_size("seq") // lengths.shape[1]
    norm_vectors = (
        lax.all_gather(ln1_gain, ("seq", "batch"), axis=0, tiled=True),
        lax.all_gather(ln1_bias, ("seq", "batch"), axis=0, tiled=True),
        lax.all_gather(out_bias, ("seq", "batch"), axis=0, tiled=True),
        lax.all_gather(ln2_gain, ("seq", "batch"), axis=0, tiled=True),
        lax.all_gather(ln2_bias, ("seq", "batch"), axis=0, tiled=True),
        lax.all_gather(proj_bias, ("seq", "batch"), axis=0, tiled=True),
    )
    gain_one, shift_one, mix_shift, gain_two, shift_two, down_shift = (
        v.astype(floaty) for v in norm_vectors
    )
    proj_in, proj_mix, proj_up, proj_down = (
        lax.all_gather(w_qkv, "seq", axis=0, tiled=True),
        lax.all_gather(w_out, "seq", axis=1, tiled=True),
        lax.all_gather(w_fc, "seq", axis=0, tiled=True),
        lax.all_gather(w_proj, "seq", axis=1, tiled=True),
    )
    own_lengths = lax.dynamic_slice_in_dim(lengths, lax.axis_index("batch"), 1, 0)
    proj_in, qv_shift, proj_mix, proj_up, up_shift, proj_down = (
        lax.all_gather(proj_in, "batch", axis=2, tiled=True),
        lax.all_gather(qv_bias, "batch", axis=1, tiled=True),
        lax.all_gather(proj_mix, "batch", axis=0, tiled=True),
        lax.all_gather(proj_up, "batch", axis=1, tiled=True),
        lax.all_gather(fc_bias, "batch", axis=0, tiled=True),
        lax.all_gather(proj_down, "batch", axis=0, tiled=True),
    )
    local_width = proj_in.shape[2]
    local_heads = local_width // head_dim
    chains = own_lengths.shape[0]
    flat_rows = chains * rows
    block_start = lax.axis_index("seq") * rows
    chain_pos = block_start + jnp.arange(rows, dtype=jnp.int32)
    key_pos = block_start - WINDOW + jnp.arange(rows + WINDOW, dtype=jnp.int32)
    own_limit = limits_of(own_lengths, chain_pos, seq_length)[0]
    valid = (chain_pos % seq_length < own_limit).astype(floaty)
    limits = limits_of(own_lengths, chain_pos, seq_length)
    mask = jax.vmap(lambda bound: allowed_keys(chain_pos, key_pos, bound, seq_length))(limits)
    inputs = tokens.astype(floaty)
    normed_f, norm_one_back = jax.vjp(layer_norm, inputs, gain_one, shift_one)
    normed = normed_f.astype(brain).reshape(flat_rows, width)
    packed = jnp.dot(
        normed, proj_in.reshape(width, 3 * local_width), preferred_element_type=floaty
    ).reshape(chains, rows, 3, local_width)
    qv_float = qv_shift.astype(floaty)
    query = (packed[:, :, 0] + qv_float[0]).astype(brain)
    key = packed[:, :, 1].astype(brain)
    value = (packed[:, :, 2] + qv_float[1]).astype(brain)
    halo_keys, halo_values = shifted((key, value), "seq", 1)
    keys = jnp.concatenate([halo_keys, key], axis=1).reshape(
        chains, rows + WINDOW, local_heads, head_dim
    )
    values = jnp.concatenate([halo_values, value], axis=1).reshape(
        chains, rows + WINDOW, local_heads, head_dim
    )
    query4 = query.reshape(chains, rows, local_heads, head_dim)
    scores = jnp.einsum("cqhd,ckhd->chqk", query4, keys, preferred_element_type=floaty) * scale
    scores = jnp.where(mask[:, None], scores, -1e30)
    top = jnp.max(scores, axis=-1, keepdims=True)
    expo = jnp.exp(scores - top)
    total = jnp.sum(expo, axis=-1, keepdims=True)
    logsum = top + jnp.log(total)
    probs = (expo / total).astype(brain)
    mixed = (
        jnp.einsum("chqk,ckhd->cqhd", probs, values, preferred_element_type=floaty)
        .reshape(flat_rows, local_width)
        .astype(brain)
    )
    branch = jnp.dot(mixed, proj_mix, preferred_element_type=floaty).reshape(chains, rows, width)
    resid = inputs + branch + mix_shift
    second_f, norm_two_back = jax.vjp(layer_norm, resid, gain_two, shift_two)
    second = second_f.astype(brain).reshape(flat_rows, width)
    pre = jnp.dot(second, proj_up, preferred_element_type=floaty) + up_shift.astype(floaty)
    active_f, gelu_back = jax.vjp(gelu_tanh, pre)
    active = active_f.astype(brain)
    ffn = jnp.dot(active, proj_down, preferred_element_type=floaty).reshape(chains, rows, width)
    result = resid + ffn + down_shift
    block_out = result.astype(brain)
    grad_out = cotangent.astype(floaty) * valid[None, :, None]
    grad_y_own = grad_out.astype(brain)
    grad_proj_bias = jnp.sum(grad_y_own.astype(floaty), axis=(0, 1))
    grad_y = grad_y_own.reshape(flat_rows, width)
    grad_w_proj = jnp.einsum("tf,td->fd", active, grad_y, preferred_element_type=floaty)
    grad_active = jnp.einsum("td,fd->tf", grad_y, proj_down, preferred_element_type=floaty)
    grad_pre = gelu_back(grad_active)[0].astype(brain)
    grad_fc_bias = bias_total(jnp.sum(grad_pre.astype(floaty), axis=0))
    grad_w_fc = jnp.einsum("td,tf->df", second, grad_pre, preferred_element_type=floaty)
    grad_second = jnp.einsum("tf,df->td", grad_pre, proj_up, preferred_element_type=floaty).reshape(
        chains, rows, width
    )
    grad_resid_norm, grad_ln2_gain, grad_ln2_bias = norm_two_back(grad_second)
    grad_resid = grad_out + grad_resid_norm
    fc_rows, proj_rows = rows_total((grad_w_fc, grad_w_proj))
    fc_rows, grad_fc_bias, proj_rows = (
        lax.psum_scatter(
            fc_rows.astype(jnp.bfloat16), "batch", scatter_dimension=1, tiled=True
        ).astype(jnp.float32),
        lax.psum_scatter(
            grad_fc_bias.astype(jnp.bfloat16), "batch", scatter_dimension=0, tiled=True
        ).astype(jnp.float32),
        lax.psum_scatter(
            proj_rows.astype(jnp.bfloat16), "batch", scatter_dimension=0, tiled=True
        ).astype(jnp.float32),
    )
    grad_branch_own = grad_resid.astype(brain)
    grad_out_bias = jnp.sum(grad_branch_own.astype(floaty), axis=(0, 1))
    grad_branch = grad_branch_own.reshape(flat_rows, width)
    grad_w_out = jnp.einsum("td,te->de", mixed, grad_branch, preferred_element_type=floaty)
    grad_mixed = jnp.einsum(
        "te,de->td", grad_branch, proj_mix, preferred_element_type=floaty
    ).astype(brain)
    grad_mixed4 = grad_mixed.reshape(chains, rows, local_heads, head_dim)
    again = jnp.einsum("cqhd,ckhd->chqk", query4, keys, preferred_element_type=floaty) * scale
    weights_f = jnp.where(mask[:, None], jnp.exp(again - logsum), 0.0)
    grad_probs = jnp.einsum("cqhd,ckhd->chqk", grad_mixed4, values, preferred_element_type=floaty)
    delta = jnp.sum(weights_f * grad_probs, axis=-1, keepdims=True)
    grad_scores = (weights_f * (grad_probs - delta)).astype(brain)
    grad_values = jnp.einsum(
        "chqk,cqhd->ckhd", weights_f.astype(brain), grad_mixed4, preferred_element_type=floaty
    ).reshape(chains, rows + WINDOW, local_width)
    grad_query = (
        (jnp.einsum("chqk,ckhd->cqhd", grad_scores, keys, preferred_element_type=floaty) * scale)
        .reshape(chains, rows, local_width)
        .astype(brain)
    )
    grad_keys = (
        jnp.einsum("chqk,cqhd->ckhd", grad_scores, query4, preferred_element_type=floaty) * scale
    ).reshape(chains, rows + WINDOW, local_width)
    back_keys, back_values = (
        shifted(grad_keys[:, :WINDOW].astype(jnp.bfloat16), "seq", -1).astype(jnp.float32),
        shifted(grad_values[:, :WINDOW].astype(jnp.bfloat16), "seq", -1).astype(jnp.float32),
    )
    own_keys = grad_keys[:, WINDOW:]
    own_values = grad_values[:, WINDOW:]
    own_keys = jnp.concatenate([own_keys[:, : rows - WINDOW], own_keys + back_keys], axis=1).astype(
        brain
    )
    own_values = jnp.concatenate(
        [own_values[:, : rows - WINDOW], own_values + back_values], axis=1
    ).astype(brain)
    grad_packed = jnp.stack([grad_query, own_keys, own_values], axis=2).reshape(
        flat_rows, 3 * local_width
    )
    grad_qv_bias = bias_total(
        jnp.stack(
            [
                jnp.sum(grad_query.astype(floaty), axis=(0, 1)),
                jnp.sum(own_values.astype(floaty), axis=(0, 1)),
            ],
            axis=0,
        )
    )
    grad_w_qkv = jnp.einsum(
        "td,te->de", normed, grad_packed, preferred_element_type=floaty
    ).reshape(width, 3, local_width)
    grad_normed = jnp.einsum(
        "te,de->td",
        grad_packed,
        proj_in.reshape(width, 3 * local_width),
        preferred_element_type=floaty,
    ).reshape(chains, rows, width)
    grad_input_norm, grad_ln1_gain, grad_ln1_bias = norm_one_back(grad_normed)
    grad_tokens = (grad_resid + grad_input_norm).astype(brain)
    qkv_rows, out_rows = rows_total((grad_w_qkv, grad_w_out))
    qkv_rows, grad_qv_bias, out_rows = (
        lax.psum_scatter(
            qkv_rows.astype(jnp.bfloat16), "batch", scatter_dimension=2, tiled=True
        ).astype(jnp.float32),
        lax.psum_scatter(
            grad_qv_bias.astype(jnp.bfloat16), "batch", scatter_dimension=1, tiled=True
        ).astype(jnp.float32),
        lax.psum_scatter(
            out_rows.astype(jnp.bfloat16), "batch", scatter_dimension=0, tiled=True
        ).astype(jnp.float32),
    )
    norm_sums = (
        lax.psum_scatter(grad_ln1_gain, ("seq", "batch"), scatter_dimension=0, tiled=True),
        lax.psum_scatter(grad_ln1_bias, ("seq", "batch"), scatter_dimension=0, tiled=True),
        lax.psum_scatter(grad_out_bias, ("seq", "batch"), scatter_dimension=0, tiled=True),
        lax.psum_scatter(grad_ln2_gain, ("seq", "batch"), scatter_dimension=0, tiled=True),
        lax.psum_scatter(grad_ln2_bias, ("seq", "batch"), scatter_dimension=0, tiled=True),
        lax.psum_scatter(grad_proj_bias, ("seq", "batch"), scatter_dimension=0, tiled=True),
    )
    return (
        block_out,
        grad_tokens,
        norm_sums[0],
        norm_sums[1],
        qkv_rows,
        grad_qv_bias,
        out_rows,
        norm_sums[2],
        norm_sums[3],
        norm_sums[4],
        fc_rows,
        grad_fc_bias,
        proj_rows,
        norm_sums[5],
    )


def solution(mesh):
    placed = (
        P("batch", "seq", None),
        P(),
        P("batch", "seq", None),
        P(("seq", "batch")),
        P(("seq", "batch")),
        P("seq", None, "batch"),
        P(None, "batch"),
        P("batch", "seq"),
        P(("seq", "batch")),
        P(("seq", "batch")),
        P(("seq", "batch")),
        P("seq", "batch"),
        P("batch"),
        P("batch", "seq"),
        P(("seq", "batch")),
    )
    return jax.shard_map(
        shards,
        mesh=mesh,
        in_specs=placed,
        out_specs=(
            P("batch", "seq", None),
            P("batch", "seq", None),
            P(("seq", "batch")),
            P(("seq", "batch")),
            P("seq", None, "batch"),
            P(None, "batch"),
            P("batch", "seq"),
            P(("seq", "batch")),
            P(("seq", "batch")),
            P(("seq", "batch")),
            P("seq", "batch"),
            P("batch"),
            P("batch", "seq"),
            P(("seq", "batch")),
        ),
        check_vma=False,
    )
```

profile of v0, /device:TPU:0, one launch (start us, length us, event | category | flops | bytes accessed | tf_op | source)
XLA Modules:
  0.0 2975.8 jit_solution(15007568904424727592)
XLA Ops:
  11.7 101.7 %all-gather.9.cloned.1.call-done = bf16[2048,3,512]{0,2,1:T(8,128)(2,1)} async-done(((bf16[256,3,512]{0,2,1:T(8,128)(2,1)}), bf16[2048,3,512]{0,2,1:T(8,128)(2,1)}) %all-gather.9.cloned.1.call-update) | async-done | bytes 6291472 | tf_op jit(solution)/shard_map/all_gather | solution.py:94
  113.4 51.3 %all-gather.13.cloned.1.call-done = bf16[512,2048]{1,0:T(8,128)(2,1)} async-done(((bf16[512,256]{1,0:T(8,128)(2,1)}), bf16[512,2048]{1,0:T(8,128)(2,1)}) %all-gather.13.cloned.1.call-update) | async-done | bytes 2097168 | tf_op jit(solution)/shard_map/all_gather | solution.py:95
  164.7 125.2 %all-gather.17.cloned.1.call-done = bf16[2048,2048]{1,0:T(8,128)(2,1)} async-done(((bf16[256,2048]{1,0:T(8,128)(2,1)}), bf16[2048,2048]{1,0:T(8,128)(2,1)}) %all-gather.17.cloned.1.call-update) | async-done | bytes 8388624 | tf_op jit(solution)/shard_map/all_gather | solution.py:96
  290.0 125.4 %all-gather.21.cloned.1.call-done = bf16[2048,2048]{1,0:T(8,128)(2,1)} async-done(((bf16[2048,256]{1,0:T(8,128)(2,1)}), bf16[2048,2048]{1,0:T(8,128)(2,1)}) %all-gather.21.cloned.1.call-update) | async-done | bytes 8388624 | tf_op jit(solution)/shard_map/all_gather | solution.py:97
  417.5 39.1 %all-reduce.14 = (bf16[2048]{0:T(1024)(128)(2,1)S(1)}, bf16[2048]{0:T(1024)(128)(2,1)S(1)}, bf16[2048]{0:T(1024)(128)(2,1)S(1)}, bf16[2048]{0:T(1024)(128)(2,1)}...) all-reduce(bf16[2048]{0:T(1024)(128)(2,1)S(1)} %dynamic-update-slic, ...), channel_id=1, replica_groups=mesh['seq'=8,'batch'=4] {'seq','batch'}, use_global_device_ids=true, to_apply=%add.1 | all-reduce | flops 12288 | bytes 49152
  456.7 6.2 all_gather.60
  463.4 5.4 all_gather.52
  470.9 99.9 %all-gather.11.cloned.1.call-done = bf16[2048,3,2048]{0,2,1:T(8,128)(2,1)} async-done(((bf16[2048,3,512]{0,2,1:T(8,128)(2,1)}), bf16[2048,3,2048]{0,2,1:T(8,128)(2,1)}) %all-gather.11.cloned.1.call-update) | async-done | bytes 25165840 | tf_op jit(solution)/shard_map/all_gather | solution.py:101
  570.8 13.9 fusion.18
  584.8 2.8 fusion.47
  587.6 4.6 collective-permute-start
  592.2 2.9 fusion.69
  595.1 3.6 collective-permute-start.1
  600.5 3.2 slice_bitcast_fusion
  605.7 3.7 copy.71
  609.3 2.9 add_convert_fusion.3
  617.3 19.5 collective-permute-done.1
  638.5 4.1 select_reduce_fusion
  647.2 4.1 fusion.50
  651.3 8.9 fusion.97
  660.6 173.1 %all-gather.19.cloned.1.call-done = bf16[2048,8192]{1,0:T(8,128)(2,1)} async-done(((bf16[2048,2048]{1,0:T(8,128)(2,1)}), bf16[2048,8192]{1,0:T(8,128)(2,1)}) %all-gather.19.cloned.1.call-update) | async-done | bytes 33554448 | tf_op jit(solution)/shard_map/all_gather | solution.py:104
  833.6 21.9 convolution_add_fusion
  855.5 181.2 %all-gather.23.cloned.1.call-done = bf16[8192,2048]{1,0:T(8,128)(2,1)} async-done(((bf16[2048,2048]{1,0:T(8,128)(2,1)}), bf16[8192,2048]{1,0:T(8,128)(2,1)}) %all-gather.23.cloned.1.call-update) | async-done | bytes 33554448 | tf_op jit(solution)/shard_map/all_gather | solution.py:106
  1036.7 21.5 fusion.99
  1058.3 17.5 fusion.45
  1081.0 5.6 convolution_convert_fusion.3
  1093.2 7.3 convolution_convert_fusion.4
  1102.8 5.8 fusion.11
  1111.4 6.3 multiply_reduce_fusion
  1117.7 4.3 multiply_convert_fusion
  1121.9 3.2 convolution_multiply_fusion
  1129.2 20.3 collective-permute-done.3
  1152.0 29.3 collective-permute-done.2
  1182.7 13.8 convolution_convert_fusion.2
  1196.6 18.4 convolution_convert_fusion
  1215.0 16.2 convolution_convert_fusion.1
  1234.7 44.1 %reduce-scatter.16.cloned.1.call-done = bf16[2048,256]{1,0:T(8,128)(2,1)} async-done(((bf16[2048,2048]{1,0:T(8,128)(2,1)}), bf16[2048,256]{1,0:T(8,128)(2,1)}) %reduce-scatter.16.cloned.1.call-update) | async-done | bytes 1048592 | tf_op jit(solution)/shard_map/reduce_scatter | solution.py:52
  1278.9 407.7 %reduce-scatter.12.cloned.1.call-done = bf16[256,3,2048]{2,0,1:T(8,128)(2,1)} async-done(((bf16[2048,3,2048]{2,0,1:T(8,128)(2,1)}), bf16[256,3,2048]{2,0,1:T(8,128)(2,1)}) %reduce-scatter.12.cloned.1.call-update) | async-done | bytes 3145744 | tf_op jit(solution)/shard_map/reduce_scatter | solution.py:49
  1686.7 546.5 %reduce-scatter.24.cloned.1.call-done = bf16[8192,256]{1,0:T(8,128)(2,1)} async-done(((bf16[8192,2048]{1,0:T(8,128)(2,1)}), bf16[8192,256]{1,0:T(8,128)(2,1)}) %reduce-scatter.24.cloned.1.call-update) | async-done | bytes 4194320 | tf_op jit(solution)/shard_map/reduce_scatter | solution.py:52
  2233.3 546.1 %reduce-scatter.20.cloned.1.call-done = bf16[256,8192]{1,0:T(8,128)(2,1)} async-done(((bf16[2048,8192]{1,0:T(8,128)(2,1)}), bf16[256,8192]{1,0:T(8,128)(2,1)}) %reduce-scatter.20.cloned.1.call-update) | async-done | bytes 4194320 | tf_op jit(solution)/shard_map/reduce_scatter | solution.py:49
  2782.4 11.5 all-reduce.11
  2793.9 19.7 fusion.29
  2815.9 11.9 fusion.36
  2829.0 38.6 %all-reduce.13 = (f32[2048]{0:T(1024)S(1)}, f32[2048]{0:T(1024)S(1)}, f32[2048]{0:T(1024)S(1)}, f32[2048]{0:T(1024)S(1)}, f32[2048]{0:T(1024)S(1)}, /*index=5*/f32[2048]{0:T(1024)S(1)}) all-reduce(f32[2048]{0:T(1024)S(1)} %get-tuple-element.16, f32[2048]{0:T(1024)S(1)} %reduce_sum.190, ...), channel_id=2, replica_groups=mesh['seq'=8,'batch'=4] {'seq','batch'}, use_global_device_ids=true, to_apply=%region_12.13.clone | all-reduce | flops 12288 | bytes 98304
  2871.2 3.9 add_convert_fusion
  2876.1 21.3 all-reduce.15
  2902.9 16.1 reduce-scatter.26.cloned.1.call-done
  2921.7 44.4 %reduce-scatter.22.cloned.1.call-done = bf16[256,2048]{1,0:T(8,128)(2,1)} async-done(((bf16[256,8192]{1,0:T(8,128)(2,1)}), bf16[256,2048]{1,0:T(8,128)(2,1)}) %reduce-scatter.22.cloned.1.call-update) | async-done | bytes 1048592 | tf_op jit(solution)/shard_map/reduce_scatter | solution.py:175
  (198 shorter events, 74.5 us)
Async XLA Ops:
  7.2 455.7 %copy-start = (s32[4,1]{0,1:T(1,128)S(1)}, s32[4,1]{0,1:T(1,128)}, u32[]{:S(2)}) copy-start(s32[4,1]{0,1:T(1,128)} %param.16) | copy-start | bytes 52
  7.2 106.1 %all-gather.9.cloned.1.call-start = ((), (), s32[]{:S(2)}) async-start(), calls=%async_computation.9 | async-start | bytes 7077888 | tf_op jit(solution)/shard_map/all_gather | solution.py:94
  9.6 155.1 %all-gather.13.cloned.1.call-start = ((), (), s32[]{:S(2)}) async-start(), calls=%async_computation.11 | async-start | bytes 2359296 | tf_op jit(solution)/shard_map/all_gather | solution.py:95
  10.3 279.6 %all-gather.17.cloned.1.call-start = ((), (), s32[]{:S(2)}) async-start(), calls=%async_computation.13 | async-start | bytes 9437184 | tf_op jit(solution)/shard_map/all_gather | solution.py:96
  11.0 404.4 %all-gather.21.cloned.1.call-start = ((), (), s32[]{:S(2)}) async-start(), calls=%async_computation.15 | async-start | bytes 9437184 | tf_op jit(solution)/shard_map/all_gather | solution.py:97
  11.6 559.2 %all-gather.11.cloned.1.call-start = ((), (), s32[]{:S(2)}) async-start(), calls=%async_computation.10 | async-start | bytes 31457280 | tf_op jit(solution)/shard_map/all_gather | solution.py:101
  113.3 538.0 %all-gather.15.cloned.1.call-start = ((), (), s32[]{:S(2)}) async-start(), calls=%async_computation.12 | async-start | bytes 10485760 | tf_op jit(solution)/shard_map/all_gather | solution.py:103
  164.7 669.0 %all-gather.19.cloned.1.call-start = ((), (), s32[]{:S(2)}) async-start(), calls=%async_computation.14 | async-start | bytes 41943040 | tf_op jit(solution)/shard_map/all_gather | solution.py:104
  290.0 746.8 %all-gather.23.cloned.1.call-start = ((), (), s32[]{:S(2)}) async-start(), calls=%async_computation.16 | async-start | bytes 41943040 | tf_op jit(solution)/shard_map/all_gather | solution.py:106
  415.5 41.2 %copy-start.24 = (bf16[2048]{0:T(1024)(128)(2,1)S(1)}, bf16[2048]{0:T(1024)(128)(2,1)}, u32[]{:S(2)}) copy-start(bf16[2048]{0:T(1024)(128)(2,1)} %param.27) | copy-start | bytes 12292
  415.5 47.9 %copy-start.26 = (bf16[2,512]{1,0:T(2,128)(2,1)S(1)}, bf16[2,512]{1,0:T(2,128)(2,1)}, u32[]{:S(2)}) copy-start(bf16[2,512]{1,0:T(2,128)(2,1)} %param.21) | copy-start | bytes 6148
  415.5 54.7 %copy-start.3 = (bf16[1,256,2048]{2,1,0:T(8,128)(2,1)S(1)}, bf16[1,256,2048]{2,1,0:T(8,128)(2,1)}, u32[]{:S(2)}) copy-start(bf16[1,256,2048]{2,1,0:T(8,128)(2,1)} %param.15) | copy-start | bytes 3145732
  415.5 863.3 %reduce-scatter.16.cloned.1.call-start = ((), (), s32[]{:S(2)}) async-start(), calls=%async_computation.19 | async-start | bytes 9437184 | tf_op jit(solution)/shard_map/reduce_scatter | solution.py:52
  470.8 113.9 %copy-start.22 = (f32[256]{0:T(256)}, f32[256]{0:T(256)S(1)}, u32[]{:S(2)}) copy-start(f32[256]{0:T(256)S(1)} %fusion.35) | copy-start | bytes 3076
  587.6 12.9 copy-start.10
  587.6 27.4 collective-permute-start
  595.1 41.7 %collective-permute-start.1 = (bf16[1,256,2048]{2,1,0:T(8,128)(2,1)}, bf16[1,256,2048]{2,1,0:T(8,128)(2,1)}, u32[]{:S(2)}, u32[]{:S(2)}) collective-permute-start(bf16[1,256,2048]{2,1,0:T(8,128)(2,1)} %get-tuple-element.39), channel_id=1, source_target_pairs={{0,4},{4,8},{8,12},{12,16},{16,20},{20,24},{24,28},{1,5},{5,9},{9,... | collective-permute-start | bytes 3145736 | tf_op jit(solution)/shard_map/ppermute | solution.py:13
  605.6 32.8 %copy-start.6 = (f32[1,256,1,2048]{1,3,2,0:T(8,128)}, f32[1,256,1,2048]{1,3,2,0:T(8,128)S(1)}, u32[]{:S(2)}) copy-start(f32[1,256,1,2048]{1,3,2,0:T(8,128)S(1)} %copy.72) | copy-start | bytes 6291460
  638.5 4.1 copy-start.15
  642.6 4.6 copy-start.2
  642.6 4.6 copy-start.19
  642.6 4.6 copy-start.20
  1086.6 600.1 %reduce-scatter.12.cloned.1.call-start = ((), (), s32[]{:S(2)}) async-start(), calls=%async_computation.17 | async-start | bytes 28311552 | tf_op jit(solution)/shard_map/reduce_scatter | solution.py:49
  1088.8 4.4 copy-start.18
  1102.7 8.6 copy-start.9
  1102.7 8.6 copy-start.12
  1102.7 14.9 slice-start
  1108.6 40.9 %copy-start.4 = (f32[16,128,512]{2,1,0:T(8,128)}, f32[16,128,512]{2,1,0:T(8,128)S(1)}, u32[]{:S(2)}) copy-start(f32[16,128,512]{2,1,0:T(8,128)S(1)} %fusion.11) | copy-start | bytes 12582916
  1109.8 7.8 slice-start.1
  1109.8 39.7 %collective-permute-start.3 = (bf16[1,256,2048]{1,2,0:T(8,128)(2,1)}, bf16[1,256,2048]{1,2,0:T(8,128)(2,1)}, u32[]{:S(2)}, u32[]{:S(2)}) collective-permute-start(bf16[1,256,2048]{1,2,0:T(8,128)(2,1)} %slice.68), channel_id=1, source_target_pairs={{4,0},{8,4},{12,8},{16,12},{20,16},{24,20},{28,24},{5,1},{9,5},{13... | collective-permute-start | bytes 3145736 | tf_op jit(solution)/shard_map/ppermute | solution.py:13
  1117.6 4.3 copy-start.7
  1121.9 4.9 copy-start.8
  1121.9 4.9 copy-start.14
  1121.9 4.9 copy-start.16
  1125.3 56.0 %collective-permute-start.2 = (bf16[1,256,2048]{1,2,0:T(8,128)(2,1)S(1)}, bf16[1,256,2048]{1,2,0:T(8,128)(2,1)S(1)}, u32[]{:S(2)}, u32[]{:S(2)}) collective-permute-start(bf16[1,256,2048]{1,2,0:T(8,128)(2,1)S(1)} %slice.69), channel_id=1, source_target_pairs={{4,0},{8,4},{12,8},{16,12},{20,16},{24,20},{28,24},{5,1},{9,5},{13... | collective-permute-start | bytes 3145736 | tf_op jit(solution)/shard_map/ppermute | solution.py:13
  1196.5 1036.7 %reduce-scatter.24.cloned.1.call-start = ((), (), s32[]{:S(2)}) async-start(), calls=%async_computation.23 | async-start | bytes 37748736 | tf_op jit(solution)/shard_map/reduce_scatter | solution.py:52
  1215.0 1564.5 %reduce-scatter.20.cloned.1.call-start = ((), (), s32[]{:S(2)}) async-start(), calls=%async_computation.21 | async-start | bytes 37748736 | tf_op jit(solution)/shard_map/reduce_scatter | solution.py:49
  1231.2 1643.9 %reduce-scatter.28.cloned.1.call-start = ((), (), s32[]{:S(2)}) async-start(), calls=%async_computation.25 | async-start | bytes 655360
  1234.7 1663.9 %reduce-scatter.18.cloned.1.call-start = ((), (), s32[]{:S(2)}) async-start(), calls=%async_computation.20 | async-start | bytes 1310720 | tf_op jit(solution)/shard_map/reduce_scatter | solution.py:252
  1278.9 1621.5 %reduce-scatter.14.cloned.1.call-start = ((), (), s32[]{:S(2)}) async-start(), calls=%async_computation.18 | async-start | bytes 3932160 | tf_op jit(solution)/shard_map/reduce_scatter | solution.py:246
  1686.7 1232.3 %reduce-scatter.26.cloned.1.call-start = ((), (), s32[]{:S(2)}) async-start(), calls=%async_computation.24 | async-start | bytes 5242880 | tf_op jit(solution)/shard_map/reduce_scatter | solution.py:181
  2233.3 546.2 %copy-start.33 = (u32[32]{0:T(128)S(1)}, u32[32]{0:T(128)}, u32[]{:S(2)}) copy-start(u32[32]{0:T(128)} %constant.159) | copy-start | bytes 388
  2233.3 546.8 %copy-start.25 = (bf16[2048]{0:T(1024)(128)(2,1)S(1)}, bf16[2048]{0:T(1024)(128)(2,1)}, u32[]{:S(2)}) copy-start(bf16[2048]{0:T(1024)(128)(2,1)} %get-tuple-element.27) | copy-start | bytes 12292
  2233.3 732.8 %reduce-scatter.22.cloned.1.call-start = ((), (), s32[]{:S(2)}) async-start(), calls=%async_computation.22 | async-start | bytes 5242880 | tf_op jit(solution)/shard_map/reduce_scatter | solution.py:175
  2793.9 19.7 copy-start.21
  2815.9 12.0 copy-start.23
  2871.2 4.9 dynamic-slice-start
  2900.4 68.5 %copy-start.1 = (s32[4,1]{0,1:T(1,128)S(1)}, s32[4,1]{0,1:T(1,128)}, u32[]{:S(2)}) copy-start(s32[4,1]{0,1:T(1,128)} %param.16) | copy-start | bytes 52
  (10 other events, 16.2 us)
Sparse Core Ops, SparseCore 0:
  10.6 102.6 all-gather.8
  115.4 49.2 all-gather.12
  166.8 123.1 all-gather.16
  291.8 123.5 all-gather.20
  416.9 153.9 all-gather.10
  572.2 58.2 all-gather.14
  632.1 201.5 all-gather.18
  835.2 201.4 all-gather.22
  1086.7 192.1 reduce-scatter.15
  1283.1 403.4 reduce-scatter.11
  1690.9 542.2 reduce-scatter.23
  2237.3 542.0 reduce-scatter.19
  2782.7 20.7 reduce-scatter.27
  2805.9 24.8 reduce-scatter.17
  2833.3 38.6 reduce-scatter.13
  2874.4 44.4 reduce-scatter.25
  2921.5 44.5 reduce-scatter.21
where the time goes:
time: 2980 us
  waiting for transfers between devices  2540 us (85%)
  matrix products  202 us (7%)
  blocking collectives  122 us (4%)
  other arithmetic  46 us (2%)
  local copies, waits for them, and re-layouts  41 us (1%)
    reduce_scatter x2, waiting for transfers between devices, rows_total(): lax.psum_scatter(pair[0].astype(jnp.bfloat16), 'seq', scatter_dimension=0...  954 us
    reduce_scatter x2, waiting for transfers between devices, rows_total(): lax.psum_scatter(pair[1].astype(jnp.bfloat16), 'seq', scatter_dimension=1...  591 us
    all_gather x1, waiting for transfers between devices, shards(): lax.all_gather(proj_down, 'batch', axis=0, tiled=True)  181 us
    all_gather x1, waiting for transfers between devices, shards(): lax.all_gather(proj_up, 'batch', axis=1, tiled=True)  173 us
    all_gather x1, waiting for transfers between devices, shards(): lax.all_gather(w_proj, 'seq', axis=1, tiled=True)  125 us
    all_gather x1, waiting for transfers between devices, shards(): lax.all_gather(w_fc, 'seq', axis=0, tiled=True)  125 us
    all_gather x1, waiting for transfers between devices, shards(): lax.all_gather(w_qkv, 'seq', axis=0, tiled=True)  102 us
    all_gather x1, waiting for transfers between devices, shards(): lax.all_gather(proj_in, 'batch', axis=2, tiled=True)  99.9 us
  transfers between devices with their start and end apart: 21, of which 17 were waited for; matrix products, arithmetic and copies ran while one was open for 8% of the time, Pallas kernels for 0%

commit v1 on v0

--- a/solution.py
+++ b/solution.py
@@ -97,13 +97,41 @@
         lax.all_gather(w_proj, "seq", axis=1, tiled=True),
     )
     own_lengths = lax.dynamic_slice_in_dim(lengths, lax.axis_index("batch"), 1, 0)
+
+    def lines_link(payload):
+        link_axis = "batch"
+        built = lax.psum(1, link_axis)
+        base_arr = lax.axis_index(link_axis)
+        part_next, near, current_block = (built, base_arr, payload.shape[0])
+        rack = [(kk, (kk + 1) % part_next) for kk in range(part_next)]
+        runs = [(kk, (kk - 1) % part_next) for kk in range(part_next)]
+        parts_out = jnp.zeros(
+            (*payload.shape[:0], part_next * current_block, *payload.shape[1:]), payload.dtype
+        )
+        parts_out = lax.dynamic_update_slice_in_dim(
+            parts_out, payload, near * current_block, axis=0
+        )
+        state_now = b_next = payload
+        v_next = part_next // 2
+        for t in [*range(1, v_next + 1)]:
+            state_now = lax.ppermute(state_now, link_axis, rack)
+            parts_out = lax.dynamic_update_slice_in_dim(
+                parts_out, state_now, (near - t) % part_next * current_block, axis=0
+            )
+            if t < part_next - v_next:
+                b_next = lax.ppermute(b_next, link_axis, runs)
+                parts_out = lax.dynamic_update_slice_in_dim(
+                    parts_out, b_next, (near + t) % part_next * current_block, axis=0
+                )
+        return parts_out
+
     proj_in, qv_shift, proj_mix, proj_up, up_shift, proj_down = (
         lax.all_gather(proj_in, "batch", axis=2, tiled=True),
         lax.all_gather(qv_bias, "batch", axis=1, tiled=True),
         lax.all_gather(proj_mix, "batch", axis=0, tiled=True),
         lax.all_gather(proj_up, "batch", axis=1, tiled=True),
         lax.all_gather(fc_bias, "batch", axis=0, tiled=True),
-        lax.all_gather(proj_down, "batch", axis=0, tiled=True),
+        lines_link(proj_down),
     )
     local_width = proj_in.shape[2]
     local_heads = local_width // head_dim

time: 2980 us -> 3120 us (1.047)
  blocking collectives: 122 us -> 344 us
  waiting for transfers between devices: 2540 us -> 2400 us
  local copies, waits for them, and re-layouts: 41 us -> 85.8 us
    ppermute x0 -> x3, waiting for transfers between devices: none -> 328 us  [the longest x2 328 us: lines_link(): state_now = lax.ppermute(state_now, link_axis, rack)]
    unnamed x3, blocking collectives: 89.2 us -> 311 us
    all_gather x1 -> x0, waiting for transfers between devices: 181 us -> none  [shards(): lax.all_gather(proj_down, 'batch', axis=0, tiled=True)]
    all_gather x1, waiting for transfers between devices: 173 us -> 0.02 us  [shards(): lax.all_gather(proj_up, 'batch', axis=1, tiled=True)]
    all_gather x1, waiting for transfers between devices: 99.9 us -> 0.01 us  [shards(): lax.all_gather(proj_in, 'batch', axis=2, tiled=True)]
    dynamic_update_slice x0 -> x4, local copies, waits for them, and re-layouts: none -> 33.2 us  [the longest x2 16.6 us: lines_link(): lax.dynamic_update_slice_in_dim(parts_out, state_now, (near - t) % part_n...]
  transfers between devices with their start and end apart: 21 -> 23, of which waited for: 17 -> 14; matrix products, arithmetic and copies ran while one was open for 8% -> 8% of each run, Pallas kernels for 0% -> 0%
where the time goes in v1:
time: 3120 us; the launch traced here: 3110 us
  waiting for transfers between devices  2400 us (77%)
  blocking collectives  344 us (11%)
  matrix products  194 us (6%)
  local copies, waits for them, and re-layouts  85.8 us (3%)
  other arithmetic  45.9 us (1%)
    reduce_scatter x2, waiting for transfers between devices, rows_total(): lax.psum_scatter(pair[0].astype(jnp.bfloat16), 'seq', scatter_dimension=0...  954 us
    reduce_scatter x2, waiting for transfers between devices, rows_total(): lax.psum_scatter(pair[1].astype(jnp.bfloat16), 'seq', scatter_dimension=1...  594 us
    ppermute x2, waiting for transfers between devices, lines_link(): state_now = lax.ppermute(state_now, link_axis, rack)  328 us
    unnamed x3, blocking collectives  311 us
    all_gather x1, waiting for transfers between devices, shards(): lax.all_gather(w_proj, 'seq', axis=1, tiled=True)  125 us
    all_gather x1, waiting for transfers between devices, shards(): lax.all_gather(w_fc, 'seq', axis=0, tiled=True)  125 us
    all_gather x1, waiting for transfers between devices, shards(): lax.all_gather(w_qkv, 'seq', axis=0, tiled=True)  102 us
    ppermute x4, waiting for transfers between devices, shifted(): lax.ppermute(value, axis, [(source, source + steps) for source in range(i...  63 us
  transfers between devices with their start and end apart: 23, of which 14 were waited for; matrix products, arithmetic and copies ran while one was open for 8% of the time, Pallas kernels for 0%

profile of v1, /device:TPU:0, one launch (start us, length us, event | category | flops | bytes accessed | tf_op | source)
XLA Modules:
  0.0 3106.0 jit_solution(245834061463324512)
XLA Ops:
  11.7 101.7 %all-gather.8.cloned.1.call-done = bf16[2048,3,512]{0,2,1:T(8,128)(2,1)} async-done(((bf16[256,3,512]{0,2,1:T(8,128)(2,1)}), bf16[2048,3,512]{0,2,1:T(8,128)(2,1)}) %all-gather.8.cloned.1.call-update) | async-done | bytes 6291472 | tf_op jit(solution)/shard_map/all_gather | solution.py:94
  113.4 51.3 %all-gather.12.cloned.1.call-done = bf16[512,2048]{1,0:T(8,128)(2,1)} async-done(((bf16[512,256]{1,0:T(8,128)(2,1)}), bf16[512,2048]{1,0:T(8,128)(2,1)}) %all-gather.12.cloned.1.call-update) | async-done | bytes 2097168 | tf_op jit(solution)/shard_map/all_gather | solution.py:95
  164.7 125.2 %all-gather.16.cloned.1.call-done = bf16[2048,2048]{1,0:T(8,128)(2,1)} async-done(((bf16[256,2048]{1,0:T(8,128)(2,1)}), bf16[2048,2048]{1,0:T(8,128)(2,1)}) %all-gather.16.cloned.1.call-update) | async-done | bytes 8388624 | tf_op jit(solution)/shard_map/all_gather | solution.py:96
  290.1 125.4 %all-gather.20.cloned.1.call-done = bf16[2048,2048]{1,0:T(8,128)(2,1)} async-done(((bf16[2048,256]{1,0:T(8,128)(2,1)}), bf16[2048,2048]{1,0:T(8,128)(2,1)}) %all-gather.20.cloned.1.call-update) | async-done | bytes 8388624 | tf_op jit(solution)/shard_map/all_gather | solution.py:97
  417.2 327.7 %collective-permute-done.2 = bf16[2048,2048]{1,0:T(8,128)(2,1)} collective-permute-done((bf16[2048,2048]{1,0:T(8,128)(2,1)}, bf16[2048,2048]{1,0:T(8,128)(2,1)}, u32[]{:S(2)}, u32[]{:S(2)}) %collective-permute-start.2) | collective-permute-done | bytes 8388640 | tf_op jit(solution)/shard_map/ppermute | solution.py:117
  748.7 261.2 %all-reduce.14 = (bf16[2048]{0:T(1024)(128)(2,1)S(1)}, bf16[2048]{0:T(1024)(128)(2,1)S(1)}, bf16[2048]{0:T(1024)(128)(2,1)S(1)}, bf16[2048]{0:T(1024)(128)(2,1)}...) all-reduce(bf16[2048]{0:T(1024)(128)(2,1)S(1)} %dynamic-update-slic, ...), channel_id=1, replica_groups=mesh['seq'=8,'batch'=4] {'seq','batch'}, use_global_device_ids=true, to_apply=%add.1 | all-reduce | flops 12288 | bytes 49152
  1010.0 6.2 all_gather.57
  1016.8 5.4 all_gather.49
  1024.6 11.1 broadcast_in_dim.48
  1035.7 8.3 constant_dynamic-update-slice_fusion.3
  1043.9 8.4 constant_dynamic-update-slice_fusion.2
  1052.3 8.4 constant_dynamic-update-slice_fusion.1
  1060.7 13.4 fusion.18
  1076.9 4.8 collective-permute-start.1
  1086.9 8.3 constant_dynamic-update-slice_fusion
  1096.7 5.4 slice_bitcast_fusion
  1104.0 3.6 copy.71
  1107.7 2.9 add_convert_fusion.3
  1110.6 15.7 collective-permute-done
  1130.1 4.0 select_reduce_fusion
  1137.7 4.1 fusion.50
  1141.8 6.2 fusion.97
  1148.4 17.3 convolution_add_fusion
  1165.6 21.5 fusion.99
  1187.1 17.5 fusion.45
  1209.9 5.6 convolution_convert_fusion.3
  1222.1 7.5 convolution_convert_fusion.4
  1231.8 5.8 fusion.11
  1240.5 6.2 multiply_reduce_fusion
  1246.7 4.2 multiply_convert_fusion
  1250.9 3.2 convolution_multiply_fusion
  1258.1 21.1 collective-permute-done.6
  1281.9 26.1 collective-permute-done.5
  1309.4 13.8 convolution_convert_fusion.2
  1323.2 16.4 convolution_convert_fusion.1
  1339.7 18.2 convolution_convert_fusion
  1361.4 47.5 %reduce-scatter.16.cloned.1.call-done = bf16[2048,256]{1,0:T(8,128)(2,1)} async-done(((bf16[2048,2048]{1,0:T(8,128)(2,1)}), bf16[2048,256]{1,0:T(8,128)(2,1)}) %reduce-scatter.16.cloned.1.call-update) | async-done | bytes 1048592 | tf_op jit(solution)/shard_map/reduce_scatter | solution.py:52
  1409.0 407.8 %reduce-scatter.12.cloned.1.call-done = bf16[256,3,2048]{2,0,1:T(8,128)(2,1)} async-done(((bf16[2048,3,2048]{2,0,1:T(8,128)(2,1)}), bf16[256,3,2048]{2,0,1:T(8,128)(2,1)}) %reduce-scatter.12.cloned.1.call-update) | async-done | bytes 3145744 | tf_op jit(solution)/shard_map/reduce_scatter | solution.py:49
  1816.9 546.5 %reduce-scatter.20.cloned.1.call-done = bf16[256,8192]{1,0:T(8,128)(2,1)} async-done(((bf16[2048,8192]{1,0:T(8,128)(2,1)}), bf16[256,8192]{1,0:T(8,128)(2,1)}) %reduce-scatter.20.cloned.1.call-update) | async-done | bytes 4194320 | tf_op jit(solution)/shard_map/reduce_scatter | solution.py:49
  2363.4 546.2 %reduce-scatter.24.cloned.1.call-done = bf16[8192,256]{1,0:T(8,128)(2,1)} async-done(((bf16[8192,2048]{1,0:T(8,128)(2,1)}), bf16[8192,256]{1,0:T(8,128)(2,1)}) %reduce-scatter.24.cloned.1.call-update) | async-done | bytes 4194320 | tf_op jit(solution)/shard_map/reduce_scatter | solution.py:52
  2912.7 11.5 all-reduce.11
  2924.2 19.7 fusion.29
  2946.2 11.9 fusion.36
  2959.3 38.6 %all-reduce.13 = (f32[2048]{0:T(1024)S(1)}, f32[2048]{0:T(1024)S(1)}, f32[2048]{0:T(1024)S(1)}, f32[2048]{0:T(1024)S(1)}, f32[2048]{0:T(1024)S(1)}, /*index=5*/f32[2048]{0:T(1024)S(1)}) all-reduce(f32[2048]{0:T(1024)S(1)} %get-tuple-element.16, f32[2048]{0:T(1024)S(1)} %reduce_sum.190, ...), channel_id=2, replica_groups=mesh['seq'=8,'batch'=4] {'seq','batch'}, use_global_device_ids=true, to_apply=%region_12.13.clone | all-reduce | flops 12288 | bytes 98304
  3001.4 3.9 add_convert_fusion
  3006.4 21.2 all-reduce.15
  3033.1 16.1 reduce-scatter.22.cloned.1.call-done
  3052.0 44.3 %reduce-scatter.26.cloned.1.call-done = bf16[2048,256]{1,0:T(8,128)(2,1)} async-done(((bf16[8192,256]{1,0:T(8,128)(2,1)}), bf16[2048,256]{1,0:T(8,128)(2,1)}) %reduce-scatter.26.cloned.1.call-update) | async-done | bytes 1048592 | tf_op jit(solution)/shard_map/reduce_scatter | solution.py:209
  (204 shorter events, 82.1 us)
Async XLA Ops:
  7.2 1009.0 %copy-start = (s32[4,1]{0,1:T(1,128)S(1)}, s32[4,1]{0,1:T(1,128)}, u32[]{:S(2)}) copy-start(s32[4,1]{0,1:T(1,128)} %param.16) | copy-start | bytes 52
  7.2 106.1 %all-gather.8.cloned.1.call-start = ((), (), s32[]{:S(2)}) async-start(), calls=%async_computation.9 | async-start | bytes 7077888 | tf_op jit(solution)/shard_map/all_gather | solution.py:94
  9.6 155.1 %all-gather.12.cloned.1.call-start = ((), (), s32[]{:S(2)}) async-start(), calls=%async_computation.11 | async-start | bytes 2359296 | tf_op jit(solution)/shard_map/all_gather | solution.py:95
  10.3 279.6 %all-gather.16.cloned.1.call-start = ((), (), s32[]{:S(2)}) async-start(), calls=%async_computation.13 | async-start | bytes 9437184 | tf_op jit(solution)/shard_map/all_gather | solution.py:96
  11.0 404.4 %all-gather.20.cloned.1.call-start = ((), (), s32[]{:S(2)}) async-start(), calls=%async_computation.15 | async-start | bytes 9437184 | tf_op jit(solution)/shard_map/all_gather | solution.py:97
  11.6 1049.0 %all-gather.10.cloned.1.call-start = ((), (), s32[]{:S(2)}) async-start(), calls=%async_computation.10 | async-start | bytes 31457280 | tf_op jit(solution)/shard_map/all_gather | solution.py:129
  113.3 1028.4 %all-gather.14.cloned.1.call-start = ((), (), s32[]{:S(2)}) async-start(), calls=%async_computation.12 | async-start | bytes 10485760 | tf_op jit(solution)/shard_map/all_gather | solution.py:131
  164.7 983.7 %all-gather.18.cloned.1.call-start = ((), (), s32[]{:S(2)}) async-start(), calls=%async_computation.14 | async-start | bytes 41943040 | tf_op jit(solution)/shard_map/all_gather | solution.py:132
  289.9 457.3 %copy-start.26 = (bf16[64]{0:T(256)(128)(2,1)S(1)}, bf16[64]{0:T(256)(128)(2,1)}, u32[]{:S(2)}) copy-start(bf16[64]{0:T(256)(128)(2,1)} %param.19) | copy-start | bytes 388
  289.9 457.5 %copy-start.27 = (bf16[64]{0:T(256)(128)(2,1)S(1)}, bf16[64]{0:T(256)(128)(2,1)}, u32[]{:S(2)}) copy-start(bf16[64]{0:T(256)(128)(2,1)} %param.18) | copy-start | bytes 388
  289.9 457.8 %copy-start.28 = (bf16[64]{0:T(256)(128)(2,1)S(1)}, bf16[64]{0:T(256)(128)(2,1)}, u32[]{:S(2)}) copy-start(bf16[64]{0:T(256)(128)(2,1)} %param.23) | copy-start | bytes 388
  289.9 458.0 %copy-start.29 = (bf16[64]{0:T(256)(128)(2,1)S(1)}, bf16[64]{0:T(256)(128)(2,1)}, u32[]{:S(2)}) copy-start(bf16[64]{0:T(256)(128)(2,1)} %param.29) | copy-start | bytes 388
  289.9 458.3 %copy-start.30 = (bf16[64]{0:T(256)(128)(2,1)S(1)}, bf16[64]{0:T(256)(128)(2,1)}, u32[]{:S(2)}) copy-start(bf16[64]{0:T(256)(128)(2,1)} %param.25) | copy-start | bytes 388
  289.9 458.5 %copy-start.31 = (bf16[64]{0:T(256)(128)(2,1)S(1)}, bf16[64]{0:T(256)(128)(2,1)}, u32[]{:S(2)}) copy-start(bf16[64]{0:T(256)(128)(2,1)} %param.24) | copy-start | bytes 388
  290.0 720.0 %copy-start.23 = (bf16[2048]{0:T(1024)(128)(2,1)S(1)}, bf16[2048]{0:T(1024)(128)(2,1)}, u32[]{:S(2)}) copy-start(bf16[2048]{0:T(1024)(128)(2,1)} %param.27) | copy-start | bytes 12292
  290.0 726.8 %copy-start.25 = (bf16[2,512]{1,0:T(2,128)(2,1)S(1)}, bf16[2,512]{1,0:T(2,128)(2,1)}, u32[]{:S(2)}) copy-start(bf16[2,512]{1,0:T(2,128)(2,1)} %param.21) | copy-start | bytes 6148
  290.0 733.5 %copy-start.3 = (bf16[1,256,2048]{2,1,0:T(8,128)(2,1)S(1)}, bf16[1,256,2048]{2,1,0:T(8,128)(2,1)}, u32[]{:S(2)}) copy-start(bf16[1,256,2048]{2,1,0:T(8,128)(2,1)} %param.15) | copy-start | bytes 3145732
  290.0 1118.9 %reduce-scatter.16.cloned.1.call-start = ((), (), s32[]{:S(2)}) async-start(), calls=%async_computation.18 | async-start | bytes 9437184 | tf_op jit(solution)/shard_map/reduce_scatter | solution.py:52
  415.4 329.4 %collective-permute-start.2 = (bf16[2048,2048]{1,0:T(8,128)(2,1)}, bf16[2048,2048]{1,0:T(8,128)(2,1)}, u32[]{:S(2)}, u32[]{:S(2)}) collective-permute-start(bf16[2048,2048]{1,0:T(8,128)(2,1)} %all-gather.20.cloned.1.call-done), channel_id=1, source_target_pairs={{0,1},{1,2},{2,3},{3,0},{4,5},{5,6},{6,7},{7,4},{8,9},{9,10},{10,1... | collective-permute-start | bytes 25165832 | tf_op jit(solution)/shard_map/ppermute | solution.py:117
  415.4 636.9 %collective-permute-start.3 = (bf16[2048,2048]{1,0:T(8,128)(2,1)}, bf16[2048,2048]{1,0:T(8,128)(2,1)}, u32[]{:S(2)}, u32[]{:S(2)}) collective-permute-start(bf16[2048,2048]{1,0:T(8,128)(2,1)} %all-gather.20.cloned.1.call-done), channel_id=1, source_target_pairs={{0,3},{1,0},{2,1},{3,2},{4,7},{5,4},{6,5},{7,6},{8,11},{9,8},{10,9... | collective-permute-start | bytes 25165832 | tf_op jit(solution)/shard_map/ppermute | solution.py:122
  744.9 342.0 %collective-permute-start.4 = (bf16[2048,2048]{1,0:T(8,128)(2,1)}, bf16[2048,2048]{1,0:T(8,128)(2,1)}, u32[]{:S(2)}, u32[]{:S(2)}) collective-permute-start(bf16[2048,2048]{1,0:T(8,128)(2,1)} %collective-permute-done.2), channel_id=1, source_target_pairs={{0,1},{1,2},{2,3},{3,0},{4,5},{5,6},{6,7},{7,4},{8,9},{9,10},{10,1... | collective-permute-start | bytes 25165832 | tf_op jit(solution)/shard_map/ppermute | solution.py:117
  1024.2 11.5 copy-start.21
  1076.9 51.7 %collective-permute-start.1 = (bf16[1,256,2048]{2,1,0:T(8,128)(2,1)}, bf16[1,256,2048]{2,1,0:T(8,128)(2,1)}, u32[]{:S(2)}, u32[]{:S(2)}) collective-permute-start(bf16[1,256,2048]{2,1,0:T(8,128)(2,1)} %get-tuple-element.39), channel_id=1, source_target_pairs={{0,4},{4,8},{8,12},{12,16},{16,20},{20,24},{24,28},{1,5},{5,9},{9,... | collective-permute-start | bytes 3145736 | tf_op jit(solution)/shard_map/ppermute | solution.py:13
  1084.4 41.9 %collective-permute-start = (bf16[1,256,2048]{2,1,0:T(8,128)(2,1)}, bf16[1,256,2048]{2,1,0:T(8,128)(2,1)}, u32[]{:S(2)}, u32[]{:S(2)}) collective-permute-start(bf16[1,256,2048]{2,1,0:T(8,128)(2,1)} %fusion.47), channel_id=1, source_target_pairs={{0,4},{4,8},{8,12},{12,16},{16,20},{20,24},{24,28},{1,5},{5,9},{9,... | collective-permute-start | bytes 3145736 | tf_op jit(solution)/shard_map/ppermute | solution.py:13
  1104.0 26.0 copy-start.6
  1204.6 5.2 copy-start.10
  1215.5 601.3 %reduce-scatter.12.cloned.1.call-start = ((), (), s32[]{:S(2)}) async-start(), calls=%async_computation.16 | async-start | bytes 28311552 | tf_op jit(solution)/shard_map/reduce_scatter | solution.py:49
  1231.8 8.6 copy-start.9
  1231.8 8.6 copy-start.11
  1231.8 14.8 slice-start
  1237.6 41.6 %copy-start.4 = (f32[16,128,512]{2,1,0:T(8,128)}, f32[16,128,512]{2,1,0:T(8,128)S(1)}, u32[]{:S(2)}) copy-start(f32[16,128,512]{2,1,0:T(8,128)S(1)} %fusion.11) | copy-start | bytes 12582916
  1238.9 7.8 slice-start.1
  1238.9 40.4 %collective-permute-start.6 = (bf16[1,256,2048]{1,2,0:T(8,128)(2,1)}, bf16[1,256,2048]{1,2,0:T(8,128)(2,1)}, u32[]{:S(2)}, u32[]{:S(2)}) collective-permute-start(bf16[1,256,2048]{1,2,0:T(8,128)(2,1)} %slice.68), channel_id=1, source_target_pairs={{4,0},{8,4},{12,8},{16,12},{20,16},{24,20},{28,24},{5,1},{9,5},{13... | collective-permute-start | bytes 3145736 | tf_op jit(solution)/shard_map/ppermute | solution.py:13
  1250.9 4.9 copy-start.15
  1254.3 53.7 %collective-permute-start.5 = (bf16[1,256,2048]{1,2,0:T(8,128)(2,1)S(1)}, bf16[1,256,2048]{1,2,0:T(8,128)(2,1)S(1)}, u32[]{:S(2)}, u32[]{:S(2)}) collective-permute-start(bf16[1,256,2048]{1,2,0:T(8,128)(2,1)S(1)} %slice.69), channel_id=1, source_target_pairs={{4,0},{8,4},{12,8},{16,12},{20,16},{24,20},{28,24},{5,1},{9,5},{13... | collective-permute-start | bytes 3145736 | tf_op jit(solution)/shard_map/ppermute | solution.py:13
  1323.2 1040.2 %reduce-scatter.20.cloned.1.call-start = ((), (), s32[]{:S(2)}) async-start(), calls=%async_computation.20 | async-start | bytes 37748736 | tf_op jit(solution)/shard_map/reduce_scatter | solution.py:49
  1339.6 1570.0 %reduce-scatter.24.cloned.1.call-start = ((), (), s32[]{:S(2)}) async-start(), calls=%async_computation.22 | async-start | bytes 37748736 | tf_op jit(solution)/shard_map/reduce_scatter | solution.py:52
  1357.9 1647.5 %reduce-scatter.28.cloned.1.call-start = ((), (), s32[]{:S(2)}) async-start(), calls=%async_computation.24 | async-start | bytes 655360
  1361.4 1667.4 %reduce-scatter.18.cloned.1.call-start = ((), (), s32[]{:S(2)}) async-start(), calls=%async_computation.19 | async-start | bytes 1310720 | tf_op jit(solution)/shard_map/reduce_scatter | solution.py:280
  1409.0 1621.6 %reduce-scatter.14.cloned.1.call-start = ((), (), s32[]{:S(2)}) async-start(), calls=%async_computation.17 | async-start | bytes 3932160 | tf_op jit(solution)/shard_map/reduce_scatter | solution.py:274
  1816.8 1232.4 %reduce-scatter.22.cloned.1.call-start = ((), (), s32[]{:S(2)}) async-start(), calls=%async_computation.21 | async-start | bytes 5242880 | tf_op jit(solution)/shard_map/reduce_scatter | solution.py:203
  2363.4 546.4 %copy-start.24 = (bf16[2048]{0:T(1024)(128)(2,1)S(1)}, bf16[2048]{0:T(1024)(128)(2,1)}, u32[]{:S(2)}) copy-start(bf16[2048]{0:T(1024)(128)(2,1)} %get-tuple-element.27) | copy-start | bytes 12292
  2363.4 546.4 %copy-start.32 = (u32[32]{0:T(128)S(1)}, u32[32]{0:T(128)}, u32[]{:S(2)}) copy-start(u32[32]{0:T(128)} %constant.185) | copy-start | bytes 388
  2363.4 732.9 %reduce-scatter.26.cloned.1.call-start = ((), (), s32[]{:S(2)}) async-start(), calls=%async_computation.23 | async-start | bytes 5242880 | tf_op jit(solution)/shard_map/reduce_scatter | solution.py:209
  2924.2 19.7 copy-start.20
  2946.2 12.0 copy-start.22
  2959.3 47.1 %dynamic-slice-start = ((bf16[8192]{0:T(1024)(128)(2,1)}, u32[]{:T(128)}), bf16[2048]{0:T(1024)(128)(2,1)S(1)}, s32[]{:S(2)}) async-start(bf16[8192]{0:T(1024)(128)(2,1)} %copy-done.20, u32[]{:T(128)} %multiply.75), calls=%async_computation.27 | async-start | bytes 8704
  3028.8 70.2 %copy-start.1 = (s32[4,1]{0,1:T(1,128)S(1)}, s32[4,1]{0,1:T(1,128)}, u32[]{:S(2)}) copy-start(s32[4,1]{0,1:T(1,128)} %param.16) | copy-start | bytes 52
  (11 other events, 39.2 us)
Sparse Core Ops, SparseCore 0:
  10.6 102.6 all-gather.7
  115.4 49.2 all-gather.11
  166.8 123.1 all-gather.15
  291.8 123.5 all-gather.19
  416.9 287.9 all-gather.9
  706.3 88.5 all-gather.13
  796.4 255.8 all-gather.17
  1215.6 193.2 reduce-scatter.15
  1413.4 403.4 reduce-scatter.11
  1820.9 542.4 reduce-scatter.19
  2367.6 542.0 reduce-scatter.23
  2912.8 20.7 reduce-scatter.27
  2936.1 24.9 reduce-scatter.17
  2963.6 38.6 reduce-scatter.13
  3004.7 44.4 reduce-scatter.21
  3051.7 44.5 reduce-scatter.25
